TPU v7x, 128 devices: a whole 4x4x4 slice. The times are simulated.
128 devices in a mesh: gx: 16 (over z, y), gy: 8 (over x, core).
Axes of the slice: x: 4, y: 4, z: 4, core: 2. Of those that a mesh axis runs over, the one named last changes fastest.
Arguments:
- state: float32 [512, 512, 128], P('gx', 'gy'), may hold values from -6 to 6
- syndromes: int32 [2, 512, 512], P(None, 'gx', 'gy'), may hold values from 0 to 1
- erased: int32 [2, 128, 128], P(None, 'gx', 'gy'), may hold values 0 or 1
- readers: int32 [16384, 1], P(('gx', 'gy')), may hold values from 0 to 127; in each aligned block of 128 rows (0 to 127, 128 to 255, ...) at most 2 rows name the same one
- conv_weight: float32 [9, 128, 128], replicated, may hold values from -0.1875 to 0.1875
- syndrome_table: float32 [2, 128], replicated, may hold values from -6 to 6
- erasure_vector: float32 [128], replicated, may hold values from -6 to 6
- read_weight: float32 [16384, 128], P(('gx', 'gy')), may hold values from -0.5 to 0.5
- erasure_offset: float32 [128], replicated, may hold values from -6 to 6
Outputs:
- final_state: float32 [512, 512, 128], P('gx', 'gy')
Inputs may be any that keep to these rules, and one draw needn't show every extreme that they name: `readers`: among the 128 blocks of one device no reader is named more than 2 times, a bound that some block reaches.
All inputs are finite; a program needn't handle non-finite values. No bound on the sum of `erased` on one device may be relied on, other than what follows from the above.
Results may differ from a plain program's by a relative error of at most 0.0003.
Values sent between devices are 32-bit elements; how exact they have to be, the bound alone decides.
No kernel may reach another device: no remote copies, remote signals or barrier semaphores. Data moves between devices by JAX's collectives and lax.ppermute only.
A program may use at most 64 MiB of HBM per device.

v0:
```python
import jax
import jax.numpy as jnp
from jax import lax
from jax.sharding import PartitionSpec as P

BS = 4
ROUNDS = 2
precise = lax.Precision.HIGHEST


def padded_2(cells, sides, width):
    for axis, dim in sides:
        count = lax.axis_size(axis)
        ends = count - 1
        head = lax.slice_in_dim(cells, 0, width, axis=dim)
        tail = lax.slice_in_dim(cells, cells.shape[dim] - width, cells.shape[dim], axis=dim)
        cells = jnp.concatenate(
            [
                lax.ppermute(tail, axis, [(i, (i + 1) % count) for i in range(ends)]),
                cells,
                lax.ppermute(head, axis, [((i + 1) % count, i) for i in range(ends)]),
            ],
            axis=dim,
        )
    return cells


def to_blocks(field, block_side):
    row_count, col_count, channels = field.shape
    block_grid = field.reshape(
        row_count // block_side, block_side, col_count // block_side, block_side, channels
    )
    return block_grid.transpose(0, 2, 1, 3, 4).reshape(
        row_count // block_side * (col_count // block_side), block_side * block_side * channels
    )


def spread_cells(values, block_rows, block_cols, block_side):
    width = values.shape[-1]
    block_grid = values.reshape(block_rows, 1, block_cols, 1, width)
    return jnp.broadcast_to(
        block_grid, (block_rows, block_side, block_cols, block_side, width)
    ).reshape(block_rows * block_side, block_cols * block_side, width)


def reader_head(payload, flag_vals, weight, offset, form):
    channels = offset.shape[0]
    lead_shape = payload.shape[:-1]
    cell_vals = payload.reshape(lead_shape + (payload.shape[-1] // channels, channels))
    mixed_vals = jnp.tanh(jnp.einsum(form, cell_vals, weight, precision=precise))
    pooled = jnp.mean(mixed_vals, axis=-2)
    return jnp.tanh(pooled + flag_vals[..., None] * offset)


def per_device(
    state,
    syndromes,
    erased,
    readers,
    conv_weight,
    syndrome_table,
    erasure_vector,
    read_weight,
    erasure_offset,
):
    tile_rows, tile_cols, channels = state.shape
    block_side = BS
    block_rows = tile_rows // block_side
    block_cols = tile_cols // block_side
    block_count = block_rows * block_cols
    gx_count = lax.axis_size("gx")
    gy_count = lax.axis_size("gy")
    device_count = gx_count * gy_count
    reader_ids = readers[:, 0]
    all_weights = lax.all_gather(read_weight, ("gx", "gy"), axis=0, tiled=True)
    block_weights = all_weights.reshape(device_count, channels, channels)[reader_ids]
    field = state
    for round_index in range(ROUNDS):
        block_flags = erased[round_index].reshape(block_count).astype(jnp.float32)
        block_states = to_blocks(field, block_side)
        corrections = reader_head(
            block_states, block_flags, block_weights, erasure_offset, "bpc,bcd->bpd"
        )
        correction_cells = spread_cells(corrections, block_rows, block_cols, block_side)
        padded = padded_2(field, (("gx", 0), ("gy", 1)), 1)
        conv_sum = jnp.zeros((tile_rows * tile_cols, channels), jnp.float32)
        for tap_index in range(9):
            row_off = tap_index // 3
            col_off = tap_index % 3
            shifted = padded[row_off : row_off + tile_rows, col_off : col_off + tile_cols].reshape(
                -1, channels
            )
            conv_sum = conv_sum + jnp.dot(
                shifted,
                conv_weight[tap_index],
                precision=precise,
                preferred_element_type=jnp.float32,
            )
        conv_sum = conv_sum.reshape(tile_rows, tile_cols, channels)
        erased_cells = spread_cells(
            erased[round_index][:, :, None], block_rows, block_cols, block_side
        )
        bits = syndromes[round_index][:, :, None]
        inputs = jnp.where(
            erased_cells > 0,
            erasure_vector,
            jnp.where(bits == 1, syndrome_table[1], syndrome_table[0]),
        )
        field = 0.5 * field + jnp.tanh(conv_sum + inputs + correction_cells)
    return field


def solution(mesh):
    placed = (
        P("gx", "gy", None),
        P(None, "gx", "gy"),
        P(None, "gx", "gy"),
        P(("gx", "gy"), None),
        P(),
        P(),
        P(),
        P(("gx", "gy"), None),
        P(),
    )
    return jax.shard_map(
        per_device, mesh=mesh, in_specs=placed, out_specs=P("gx", "gy", None), check_vma=False
    )
```

profile of v0, /device:TPU:33, one launch (start us, length us, event | category | flops | bytes accessed | tf_op | source)
XLA Modules:
  0.0 146.4 jit_solution(11949596468125509112)
XLA Ops:
  6.5 0.7 all-gather.2.cloned.1.call-update
  7.3 0.8 fusion.57
  8.0 3.2 %collective-permute-start = (f32[1,64,128]{2,1,0:T(8,128)S(1)}, f32[1,64,128]{2,1,0:T(8,128)S(1)}, u32[]{:S(2)}, u32[]{:S(2)}) collective-permute-start(f32[1,64,128]{2,1,0:T(8,128)S(1)} %get-tuple-element.34), channel_id=1, source_target_pairs={{0,8},{8,16},{16,24},{24,32},{32,40},{40,48},{48,56},{56,64},{64,7... | collective-permute-start | bytes 98312 | tf_op jit(solution)/shard_map/ppermute | solution.py:19
  11.2 4.2 %collective-permute-start.1 = (f32[1,64,128]{2,1,0:T(8,128)S(1)}, f32[1,64,128]{2,1,0:T(8,128)S(1)}, u32[]{:S(2)}, u32[]{:S(2)}) collective-permute-start(f32[1,64,128]{2,1,0:T(8,128)S(1)} %get-tuple-element.33), channel_id=1, source_target_pairs={{8,0},{16,8},{24,16},{32,24},{40,32},{48,40},{56,48},{64,56},{72,6... | collective-permute-start | bytes 98312 | tf_op jit(solution)/shard_map/ppermute | solution.py:21
  15.4 0.7 fusion.52
  16.1 0.8 slice_bitcast_fusion.1
  16.9 0.7 compare_bitcast_fusion
  17.6 0.8 convert_bitcast_fusion
  18.4 0.7 fusion.51
  19.1 1.4 copy.12
  20.5 0.1 broadcast_in_dim.66
  20.6 0.2 gt.32
  20.8 0.1 broadcast_in_dim.73
  20.9 0.2 gt.35
  21.1 0.0 collective-permute-done
  21.1 0.0 copy-start.2
  21.1 0.4 pad_maximum_fusion.6
  21.5 4.2 %collective-permute-start.2 = (f32[34,1,128]{2,1,0:T(1,128)S(1)}, f32[34,1,128]{2,1,0:T(1,128)S(1)}, u32[]{:S(2)}, u32[]{:S(2)}) collective-permute-start(f32[34,1,128]{2,1,0:T(1,128)S(1)} %get-tuple-element.24), channel_id=1, source_target_pairs={{0,1},{1,2},{2,3},{3,4},{4,5},{5,6},{6,7},{8,9},{9,10},{10,11},{11... | collective-permute-start | bytes 52232 | tf_op jit(solution)/shard_map/ppermute | solution.py:19
  25.8 1.9 %collective-permute-start.3 = (f32[34,1,128]{2,1,0:T(1,128)S(1)}, f32[34,1,128]{2,1,0:T(1,128)S(1)}, u32[]{:S(2)}, u32[]{:S(2)}) collective-permute-start(f32[34,1,128]{2,1,0:T(1,128)S(1)} %get-tuple-element.25), channel_id=1, source_target_pairs={{1,0},{2,1},{3,2},{4,3},{5,4},{6,5},{7,6},{9,8},{10,9},{11,10},{12... | collective-permute-start | bytes 52232 | tf_op jit(solution)/shard_map/ppermute | solution.py:21
  27.7 1.0 fusion.14
  28.7 1.0 fusion.28
  29.7 1.6 %collective-permute-done.3 = f32[34,1,128]{2,1,0:T(1,128)S(1)} collective-permute-done((f32[34,1,128]{2,1,0:T(1,128)S(1)}, f32[34,1,128]{2,1,0:T(1,128)S(1)}, u32[]{:S(2)}, u32[]{:S(2)}) %collective-permute-start.3) | collective-permute-done | bytes 17440 | tf_op jit(solution)/shard_map/ppermute | solution.py:21
  31.3 0.9 pad_maximum_fusion.5
  32.2 1.0 fusion.11
  33.2 1.0 convolution_add_fusion.12
  34.2 1.0 convolution_add_fusion.11
  35.2 1.0 convolution_add_fusion.10
  36.2 1.0 convolution_add_fusion.9
  37.2 1.0 convolution_add_fusion.8
  38.2 1.1 fusion.2
  39.2 41.7 %all-gather.2.cloned.1.call-done = f32[16384,128]{1,0:T(8,128)} async-done(((f32[128,128]{1,0:T(8,128)}), f32[16384,128]{1,0:T(8,128)}) %all-gather.2.cloned.1.call-update) | async-done | bytes 8388624 | tf_op jit(solution)/shard_map/all_gather | solution.py:75
  81.0 7.7 %gather_fusion = f32[128,128,128]{2,1,0:T(8,128)} fusion(f32[128,128,128]{2,1,0:T(8,128)} %bitcast.126, s32[1024]{0:T(1024)S(1)} %pad_clamp_fusion), kind=kCustom, calls=%fused_computation | custom fusion | bytes 16777728 | tf_op jit(solution)/shard_map/gather | solution.py:76
  88.7 10.5 %fusion.3 = f32[128,128]{1,0:T(8,128)S(1)} fusion(f32[128,128,128]{2,1,0:T(8,128)} %gather_fusion, f32[128,16,128]{2,1,0:T(8,128)S(1)} %bitcast.132), kind=kOutput, calls=%fused_computation.29 | convolution fusion | flops 402898944 | bytes 9502720 | tf_op jit(solution)/shard_map/bpc,bcd->bpd/dot_general | solution.py:50
  99.2 0.0 copy-start.5
  99.2 0.1 add_tanh_fusion.1
  99.3 0.2 broadcast_in_dim.72
  99.6 0.3 copy-done.5
  99.9 0.7 tanh_add_fusion.1
  100.6 0.2 copy.13
  100.8 7.4 %fusion.4 = f32[128,128]{1,0:T(8,128)S(1)} fusion(f32[128,16,128]{2,1,0:T(8,128)S(1)} %bitcast.137, f32[128,128,128]{2,1,0:T(8,128)S(1)} %copy-done), kind=kOutput, calls=%fused_computation.30 | convolution fusion | flops 402898944 | bytes 9502720 | tf_op jit(solution)/shard_map/bpc,bcd->bpd/dot_general | solution.py:50
  108.2 4.4 %collective-permute-start.5 = (f32[1,64,128]{2,1,0:T(8,128)S(1)}, f32[1,64,128]{2,1,0:T(8,128)S(1)}, u32[]{:S(2)}, u32[]{:S(2)}) collective-permute-start(f32[1,64,128]{2,1,0:T(8,128)S(1)} %get-tuple-element.29), channel_id=1, source_target_pairs={{8,0},{16,8},{24,16},{32,24},{40,32},{48,40},{56,48},{64,56},{72,6... | collective-permute-start | bytes 98312 | tf_op jit(solution)/shard_map/ppermute | solution.py:21
  112.6 1.9 %collective-permute-start.4 = (f32[1,64,128]{2,1,0:T(8,128)S(1)}, f32[1,64,128]{2,1,0:T(8,128)S(1)}, u32[]{:S(2)}, u32[]{:S(2)}) collective-permute-start(f32[1,64,128]{2,1,0:T(8,128)S(1)} %get-tuple-element.28), channel_id=1, source_target_pairs={{0,8},{8,16},{16,24},{24,32},{32,40},{40,48},{48,56},{56,64},{64,7... | collective-permute-start | bytes 98312 | tf_op jit(solution)/shard_map/ppermute | solution.py:19
  114.5 0.1 add_tanh_fusion
  114.6 0.0 collective-permute-done.5
  114.6 4.7 %collective-permute-done.4 = f32[1,64,128]{2,1,0:T(8,128)S(1)} collective-permute-done((f32[1,64,128]{2,1,0:T(8,128)S(1)}, f32[1,64,128]{2,1,0:T(8,128)S(1)}, u32[]{:S(2)}, u32[]{:S(2)}) %collective-permute-start.4) | collective-permute-done | bytes 32800 | tf_op jit(solution)/shard_map/ppermute | solution.py:19
  119.4 4.2 %collective-permute-start.6 = (f32[34,1,128]{2,1,0:T(1,128)S(1)}, f32[34,1,128]{2,1,0:T(1,128)S(1)}, u32[]{:S(2)}, u32[]{:S(2)}) collective-permute-start(f32[34,1,128]{2,1,0:T(1,128)S(1)} %get-tuple-element.19), channel_id=1, source_target_pairs={{0,1},{1,2},{2,3},{3,4},{4,5},{5,6},{6,7},{8,9},{9,10},{10,11},{11... | collective-permute-start | bytes 52232 | tf_op jit(solution)/shard_map/ppermute | solution.py:19
  123.6 0.0 copy-start.3
  123.6 2.1 %collective-permute-start.7 = (f32[34,1,128]{2,1,0:T(1,128)S(1)}, f32[34,1,128]{2,1,0:T(1,128)S(1)}, u32[]{:S(2)}, u32[]{:S(2)}) collective-permute-start(f32[34,1,128]{2,1,0:T(1,128)S(1)} %get-tuple-element.20), channel_id=1, source_target_pairs={{1,0},{2,1},{3,2},{4,3},{5,4},{6,5},{7,6},{9,8},{10,9},{11,10},{12... | collective-permute-start | bytes 52232 | tf_op jit(solution)/shard_map/ppermute | solution.py:21
  125.6 0.2 pad_maximum_fusion.1
  125.9 1.0 fusion.26
  126.9 0.0 collective-permute-done.6
  126.9 1.9 %collective-permute-done.7 = f32[34,1,128]{2,1,0:T(1,128)S(1)} collective-permute-done((f32[34,1,128]{2,1,0:T(1,128)S(1)}, f32[34,1,128]{2,1,0:T(1,128)S(1)}, u32[]{:S(2)}, u32[]{:S(2)}) %collective-permute-start.7) | collective-permute-done | bytes 17440 | tf_op jit(solution)/shard_map/ppermute | solution.py:21
  128.8 0.2 maximum_maximum_fusion
  129.0 0.8 fusion.53
  129.8 1.0 fusion.9
  130.8 1.0 convolution_add_fusion.6
  131.8 1.0 convolution_add_fusion.5
  132.8 1.0 convolution_add_fusion.4
  133.7 1.0 convolution_add_fusion.3
  134.7 1.0 convolution_add_fusion.2
  135.7 1.0 convolution_add_fusion.1
  136.7 1.1 fusion
  137.8 0.2 broadcast_in_dim.76
  138.0 1.5 %tanh_add_fusion = f32[32,64,128]{2,1,0:T(8,128)} fusion(f32[32,64,128]{2,1,0:T(8,128)S(1)} %bitcast.134, f32[32,64,128]{2,1,0:T(8,128)S(1)} %bitcast.144, f32[32,64,128]{2,1,0:T(8,128)S(1)} %tanh_add_fusion.1, f32[128]{0:T(128)S(1)} %get-tuple-element.42, f32[128]{0:T(128)S(1)} %get-tuple-element.41, f32[128]{0:T(128)S(1)} %copy-done.5, ...), kind=kLoop, calls=%fused_computation.41 | loop fusion | flops 1572864 | bytes 4199936 | tf_op jit(solution)/shard_map/add | solution.py:109
  (19 shorter events, 0.1 us)
Async XLA Ops:
  6.5 74.4 %all-gather.2.cloned.1.call-start = ((), (), s32[]{:S(2)}) async-start(), calls=%async_computation | async-start | bytes 8454144 | tf_op jit(solution)/shard_map/all_gather | solution.py:75
  8.0 13.0 %collective-permute-start = (f32[1,64,128]{2,1,0:T(8,128)S(1)}, f32[1,64,128]{2,1,0:T(8,128)S(1)}, u32[]{:S(2)}, u32[]{:S(2)}) collective-permute-start(f32[1,64,128]{2,1,0:T(8,128)S(1)} %get-tuple-element.34), channel_id=1, source_target_pairs={{0,8},{8,16},{16,24},{24,32},{32,40},{40,48},{48,56},{56,64},{64,7... | collective-permute-start | bytes 98312 | tf_op jit(solution)/shard_map/ppermute | solution.py:19
  11.2 9.8 %collective-permute-start.1 = (f32[1,64,128]{2,1,0:T(8,128)S(1)}, f32[1,64,128]{2,1,0:T(8,128)S(1)}, u32[]{:S(2)}, u32[]{:S(2)}) collective-permute-start(f32[1,64,128]{2,1,0:T(8,128)S(1)} %get-tuple-element.33), channel_id=1, source_target_pairs={{8,0},{16,8},{24,16},{32,24},{40,32},{48,40},{56,48},{64,56},{72,6... | collective-permute-start | bytes 98312 | tf_op jit(solution)/shard_map/ppermute | solution.py:21
  17.6 3.5 %copy-start.1 = (f32[32,64,128]{2,1,0:T(8,128)S(1)}, f32[32,64,128]{2,1,0:T(8,128)}, u32[]{:S(2)}) copy-start(f32[32,64,128]{2,1,0:T(8,128)} %param.9) | copy-start | bytes 3145732
  21.1 6.6 %copy-start.2 = (f32[9,128,128]{2,1,0:T(8,128)S(1)}, f32[9,128,128]{2,1,0:T(8,128)}, u32[]{:S(2)}) copy-start(f32[9,128,128]{2,1,0:T(8,128)} %param.13) | copy-start | bytes 1769476
  21.5 8.2 %collective-permute-start.2 = (f32[34,1,128]{2,1,0:T(1,128)S(1)}, f32[34,1,128]{2,1,0:T(1,128)S(1)}, u32[]{:S(2)}, u32[]{:S(2)}) collective-permute-start(f32[34,1,128]{2,1,0:T(1,128)S(1)} %get-tuple-element.24), channel_id=1, source_target_pairs={{0,1},{1,2},{2,3},{3,4},{4,5},{5,6},{6,7},{8,9},{9,10},{10,11},{11... | collective-permute-start | bytes 52232 | tf_op jit(solution)/shard_map/ppermute | solution.py:19
  25.8 5.5 %collective-permute-start.3 = (f32[34,1,128]{2,1,0:T(1,128)S(1)}, f32[34,1,128]{2,1,0:T(1,128)S(1)}, u32[]{:S(2)}, u32[]{:S(2)}) collective-permute-start(f32[34,1,128]{2,1,0:T(1,128)S(1)} %get-tuple-element.25), channel_id=1, source_target_pairs={{1,0},{2,1},{3,2},{4,3},{5,4},{6,5},{7,6},{9,8},{10,9},{11,10},{12... | collective-permute-start | bytes 52232 | tf_op jit(solution)/shard_map/ppermute | solution.py:21
  88.7 10.6 %copy-start.4 = (f32[128]{0:T(128)S(1)}, f32[128]{0:T(128)}, u32[]{:S(2)}) copy-start(f32[128]{0:T(128)} %param.17) | copy-start | bytes 1540
  88.7 12.2 %copy-start = (f32[128,128,128]{2,1,0:T(8,128)S(1)}, f32[128,128,128]{2,1,0:T(8,128)}, u32[]{:S(2)}) copy-start(f32[128,128,128]{2,1,0:T(8,128)} %gather_fusion) | copy-start | bytes 25165828
  99.2 0.7 copy-start.5
  108.2 6.4 %collective-permute-start.5 = (f32[1,64,128]{2,1,0:T(8,128)S(1)}, f32[1,64,128]{2,1,0:T(8,128)S(1)}, u32[]{:S(2)}, u32[]{:S(2)}) collective-permute-start(f32[1,64,128]{2,1,0:T(8,128)S(1)} %get-tuple-element.29), channel_id=1, source_target_pairs={{8,0},{16,8},{24,16},{32,24},{40,32},{48,40},{56,48},{64,56},{72,6... | collective-permute-start | bytes 98312 | tf_op jit(solution)/shard_map/ppermute | solution.py:21
  112.6 6.8 %collective-permute-start.4 = (f32[1,64,128]{2,1,0:T(8,128)S(1)}, f32[1,64,128]{2,1,0:T(8,128)S(1)}, u32[]{:S(2)}, u32[]{:S(2)}) collective-permute-start(f32[1,64,128]{2,1,0:T(8,128)S(1)} %get-tuple-element.28), channel_id=1, source_target_pairs={{0,8},{8,16},{16,24},{24,32},{32,40},{40,48},{48,56},{56,64},{64,7... | collective-permute-start | bytes 98312 | tf_op jit(solution)/shard_map/ppermute | solution.py:19
  119.4 7.5 %collective-permute-start.6 = (f32[34,1,128]{2,1,0:T(1,128)S(1)}, f32[34,1,128]{2,1,0:T(1,128)S(1)}, u32[]{:S(2)}, u32[]{:S(2)}) collective-permute-start(f32[34,1,128]{2,1,0:T(1,128)S(1)} %get-tuple-element.19), channel_id=1, source_target_pairs={{0,1},{1,2},{2,3},{3,4},{4,5},{5,6},{6,7},{8,9},{9,10},{10,11},{11... | collective-permute-start | bytes 52232 | tf_op jit(solution)/shard_map/ppermute | solution.py:19
  123.6 2.3 %copy-start.3 = (f32[9,128,128]{2,1,0:T(8,128)S(1)}, f32[9,128,128]{2,1,0:T(8,128)}, u32[]{:S(2)}) copy-start(f32[9,128,128]{2,1,0:T(8,128)} %param.13) | copy-start | bytes 1769476
  123.6 5.2 %collective-permute-start.7 = (f32[34,1,128]{2,1,0:T(1,128)S(1)}, f32[34,1,128]{2,1,0:T(1,128)S(1)}, u32[]{:S(2)}, u32[]{:S(2)}) collective-permute-start(f32[34,1,128]{2,1,0:T(1,128)S(1)} %get-tuple-element.20), channel_id=1, source_target_pairs={{1,0},{2,1},{3,2},{4,3},{5,4},{6,5},{7,6},{9,8},{10,9},{11,10},{12... | collective-permute-start | bytes 52232 | tf_op jit(solution)/shard_map/ppermute | solution.py:21
Sparse Core Ops, SparseCore 0:
  10.3 70.6 all-gather.1
where the time goes:
time: 147 us; the launch traced here: 146 us
  waiting for transfers between devices  50.7 us (34%)
  matrix products  35.7 us (24%)
  starting transfers between devices  26 us (18%)
  between operations  13.9 us (9%)
  local copies, waits for them, and re-layouts  13 us (9%)
  other arithmetic  7.12 us (5%)
    all_gather x1, waiting for transfers between devices, per_device(): all_weights = lax.all_gather(read_weight, ('gx', 'gy'), axis=0, tiled=True)  41.7 us
    dot_general x2, matrix products, reader_head(): jnp.einsum(form, cell_vals, weight, precision=precise)  17.9 us
    dot_general x18, matrix products, per_device(): jnp.dot(shifted, conv_weight[tap_index], precision=precise, preferred_ele...  17.8 us
    ppermute x4, starting transfers between devices, padded_2(): lax.ppermute(tail, axis, [(i, (i + 1) % count) for i in range(ends)])  13.5 us
    ppermute x4, starting transfers between devices, padded_2(): lax.ppermute(head, axis, [((i + 1) % count, i) for i in range(ends)])  12.5 us
    gather x1, local copies, waits for them, and re-layouts, per_device(): all_weights.reshape(device_count, channels, channels)[reader_ids]  7.68 us
    ppermute x4, waiting for transfers between devices, padded_2(): lax.ppermute(tail, axis, [(i, (i + 1) % count) for i in range(ends)])  4.74 us
    ppermute x4, waiting for transfers between devices, padded_2(): lax.ppermute(head, axis, [((i + 1) % count, i) for i in range(ends)])  3.48 us
  transfers between devices with their start and end apart: 9, of which 4 were waited for; matrix products, arithmetic and copies ran while one was open for 12% of the time, Pallas kernels for 0%

commit v1 on v0

--- a/solution.py
+++ b/solution.py
@@ -72,7 +72,10 @@
     gy_count = lax.axis_size("gy")
     device_count = gx_count * gy_count
     reader_ids = readers[:, 0]
-    all_weights = lax.all_gather(read_weight, ("gx", "gy"), axis=0, tiled=True)
+    all_weights = jnp.concatenate(
+        lax.all_to_all(jnp.stack([read_weight] * lax.axis_size(("gx", "gy"))), ("gx", "gy"), 0, 0),
+        axis=0,
+    )
     block_weights = all_weights.reshape(device_count, channels, channels)[reader_ids]
     field = state
     for round_index in range(ROUNDS):

time: 147 us -> 184 us (1.25)
  waiting for transfers between devices: 50.7 us -> 84.1 us
  starting transfers between devices: 26 us -> 42.1 us
  between operations: 13.9 us -> 0.59 us
  other arithmetic: 7.12 us -> 4.16 us
  local copies, waits for them, and re-layouts: 13 us -> 15.3 us
    ppermute x4, waiting for transfers between devices: 4.74 us -> 79.7 us  [padded_2(): lax.ppermute(tail, axis, [(i, (i + 1) % count) for i in range(ends)])]
    all_gather x1 -> x0, waiting for transfers between devices: 41.7 us -> none  [per_device(): all_weights = lax.all_gather(read_weight, ('gx', 'gy'), axis=0, tiled=True)]
    all_to_all x0 -> x1, starting transfers between devices: none -> 11 us  [per_device(): lax.all_to_all(jnp.stack([read_weight] * lax.axis_size(('gx', 'gy'))), ('...]
    another operation x0 -> x1, local copies, waits for them, and re-layouts: none -> 5.1 us  [per_device(): jnp.stack([read_weight] * lax.axis_size(('gx', 'gy')))]
    ppermute x4, starting transfers between devices: 13.5 us -> 17.5 us  [padded_2(): lax.ppermute(tail, axis, [(i, (i + 1) % count) for i in range(ends)])]
  transfers between devices with their start and end apart: 9 -> 9, of which waited for: 4 -> 4; matrix products, arithmetic and copies ran while one was open for 12% -> 11% of each run, Pallas kernels for 0% -> 0%
where the time goes in v1:
time: 184 us; the launch traced here: 182 us
  waiting for transfers between devices  84.1 us (46%)
  starting transfers between devices  42.1 us (23%)
  matrix products  35.8 us (19%)
  local copies, waits for them, and re-layouts  15.3 us (8%)
  other arithmetic  4.16 us (2%)
    ppermute x4, waiting for transfers between devices, padded_2(): lax.ppermute(tail, axis, [(i, (i + 1) % count) for i in range(ends)])  79.7 us
    dot_general x2, matrix products, reader_head(): jnp.einsum(form, cell_vals, weight, precision=precise)  18 us
    dot_general x18, matrix products, per_device(): jnp.dot(shifted, conv_weight[tap_index], precision=precise, preferred_ele...  17.8 us
    ppermute x4, starting transfers between devices, padded_2(): lax.ppermute(tail, axis, [(i, (i + 1) % count) for i in range(ends)])  17.5 us
    ppermute x4, starting transfers between devices, padded_2(): lax.ppermute(head, axis, [((i + 1) % count, i) for i in range(ends)])  13.7 us
    all_to_all x1, starting transfers between devices, per_device(): lax.all_to_all(jnp.stack([read_weight] * lax.axis_size(('gx', 'gy'))), ('...  11 us
    gather x1, local copies, waits for them, and re-layouts, per_device(): all_weights.reshape(device_count, channels, channels)[reader_ids]  7.68 us
    another operation x1, local copies, waits for them, and re-layouts, per_device(): jnp.stack([read_weight] * lax.axis_size(('gx', 'gy')))  5.1 us
  transfers between devices with their start and end apart: 9, of which 4 were waited for; matrix products, arithmetic and copies ran while one was open for 11% of the time, Pallas kernels for 0%

profile of v1, /device:TPU:33, one launch (start us, length us, event | category | flops | bytes accessed | tf_op | source)
XLA Modules:
  0.0 182.0 jit_solution(9173233125770669361)
XLA Ops:
  0.0 5.1 %stack.2 = f32[128,128,128]{2,1,0:T(8,128)} broadcast(f32[128,128]{1,0:T(8,128)} %param.16), dimensions={1,2} | broadcast | bytes 8454144 | tf_op jit(solution)/shard_map/stack | solution.py:76
  5.1 0.0 copy-start.4
  5.1 11.0 %all-to-all-start = ((f32[128,128,128]{2,1,0:T(8,128)}), f32[128,128,128]{2,1,0:T(8,128)}, u32[]{:S(2)}, u32[]{:S(2)}) async-start(f32[128,128,128]{2,1,0:T(8,128)} %stack.2), calls=%async_computation | async-start | bytes 16777216 | tf_op jit(solution)/shard_map/all_to_all | solution.py:76
  16.1 0.0 copy-done.1
  16.1 4.2 %collective-permute-start.1 = (f32[1,64,128]{2,1,0:T(8,128)S(1)}, f32[1,64,128]{2,1,0:T(8,128)S(1)}, u32[]{:S(2)}, u32[]{:S(2)}) collective-permute-start(f32[1,64,128]{2,1,0:T(8,128)S(1)} %get-tuple-element.33), channel_id=1, source_target_pairs={{8,0},{16,8},{24,16},{32,24},{40,32},{48,40},{56,48},{64,56},{72,6... | collective-permute-start | bytes 98312 | tf_op jit(solution)/shard_map/ppermute | solution.py:21
  20.4 1.9 %collective-permute-start = (f32[1,64,128]{2,1,0:T(8,128)S(1)}, f32[1,64,128]{2,1,0:T(8,128)S(1)}, u32[]{:S(2)}, u32[]{:S(2)}) collective-permute-start(f32[1,64,128]{2,1,0:T(8,128)S(1)} %get-tuple-element.34), channel_id=1, source_target_pairs={{0,8},{8,16},{16,24},{24,32},{32,40},{40,48},{48,56},{56,64},{64,7... | collective-permute-start | bytes 98312 | tf_op jit(solution)/shard_map/ppermute | solution.py:19
  22.3 0.0 copy-done.9
  22.3 0.0 copy-done.8
  22.4 0.1 broadcast_in_dim.73
  22.5 0.2 gt.35
  22.7 0.1 broadcast_in_dim.66
  22.8 0.2 gt.32
  22.9 0.2 copy.12
  23.1 79.7 %collective-permute-done = f32[1,64,128]{2,1,0:T(8,128)S(1)} collective-permute-done((f32[1,64,128]{2,1,0:T(8,128)S(1)}, f32[1,64,128]{2,1,0:T(8,128)S(1)}, u32[]{:S(2)}, u32[]{:S(2)}) %collective-permute-start) | collective-permute-done | bytes 32800 | tf_op jit(solution)/shard_map/ppermute | solution.py:19
  102.9 1.3 collective-permute-done.1
  104.1 0.3 pad_maximum_fusion.6
  104.5 9.8 %collective-permute-start.2 = (f32[34,1,128]{2,1,0:T(1,128)S(1)}, f32[34,1,128]{2,1,0:T(1,128)S(1)}, u32[]{:S(2)}, u32[]{:S(2)}) collective-permute-start(f32[34,1,128]{2,1,0:T(1,128)S(1)} %get-tuple-element.24), channel_id=1, source_target_pairs={{0,1},{1,2},{2,3},{3,4},{4,5},{5,6},{6,7},{8,9},{9,10},{10,11},{11... | collective-permute-start | bytes 52232 | tf_op jit(solution)/shard_map/ppermute | solution.py:19
  114.3 2.1 %collective-permute-start.3 = (f32[34,1,128]{2,1,0:T(1,128)S(1)}, f32[34,1,128]{2,1,0:T(1,128)S(1)}, u32[]{:S(2)}, u32[]{:S(2)}) collective-permute-start(f32[34,1,128]{2,1,0:T(1,128)S(1)} %get-tuple-element.25), channel_id=1, source_target_pairs={{1,0},{2,1},{3,2},{4,3},{5,4},{6,5},{7,6},{9,8},{10,9},{11,10},{12... | collective-permute-start | bytes 52232 | tf_op jit(solution)/shard_map/ppermute | solution.py:21
  116.4 1.0 fusion.28
  117.4 1.0 fusion.14
  118.4 0.0 collective-permute-done.2
  118.4 1.0 collective-permute-done.3
  119.4 0.9 pad_maximum_fusion.5
  120.3 1.0 fusion.11
  121.3 1.0 convolution_add_fusion.12
  122.3 1.0 convolution_add_fusion.11
  123.3 1.0 convolution_add_fusion.10
  124.2 1.0 convolution_add_fusion.9
  125.2 1.0 convolution_add_fusion.8
  126.2 1.1 fusion.2
  127.3 0.0 all-to-all-done
  127.3 7.7 %gather_fusion = f32[128,128,128]{2,1,0:T(8,128)} fusion(f32[128,128,128]{2,1,0:T(8,128)} %all-to-all-done, s32[1024]{0:T(1024)S(1)} %pad_clamp_fusion), kind=kCustom, calls=%fused_computation | custom fusion | bytes 16777728 | tf_op jit(solution)/shard_map/gather | solution.py:79
  135.0 10.6 %fusion.3 = f32[128,128]{1,0:T(8,128)S(1)} fusion(f32[128,128,128]{2,1,0:T(8,128)} %gather_fusion, f32[128,16,128]{2,1,0:T(8,128)S(1)} %bitcast.130), kind=kOutput, calls=%fused_computation.29 | convolution fusion | flops 402898944 | bytes 9502720 | tf_op jit(solution)/shard_map/bpc,bcd->bpd/dot_general | solution.py:50
  145.6 0.0 copy-start.7
  145.6 0.1 add_tanh_fusion.1
  145.7 0.2 broadcast_in_dim.72
  146.0 0.3 copy-done.7
  146.2 0.7 tanh_add_fusion.1
  147.0 2.1 %collective-permute-start.4 = (f32[1,64,128]{2,1,0:T(8,128)S(1)}, f32[1,64,128]{2,1,0:T(8,128)S(1)}, u32[]{:S(2)}, u32[]{:S(2)}) collective-permute-start(f32[1,64,128]{2,1,0:T(8,128)S(1)} %get-tuple-element.28), channel_id=1, source_target_pairs={{0,8},{8,16},{16,24},{24,32},{32,40},{40,48},{48,56},{56,64},{64,7... | collective-permute-start | bytes 98312 | tf_op jit(solution)/shard_map/ppermute | solution.py:19
  149.1 5.3 %collective-permute-start.5 = (f32[1,64,128]{2,1,0:T(8,128)S(1)}, f32[1,64,128]{2,1,0:T(8,128)S(1)}, u32[]{:S(2)}, u32[]{:S(2)}) collective-permute-start(f32[1,64,128]{2,1,0:T(8,128)S(1)} %get-tuple-element.29), channel_id=1, source_target_pairs={{8,0},{16,8},{24,16},{32,24},{40,32},{48,40},{56,48},{64,56},{72,6... | collective-permute-start | bytes 98312 | tf_op jit(solution)/shard_map/ppermute | solution.py:21
  154.4 0.2 copy.13
  154.6 7.4 %fusion.4 = f32[128,128]{1,0:T(8,128)S(1)} fusion(f32[128,16,128]{2,1,0:T(8,128)S(1)} %bitcast.135, f32[128,128,128]{2,1,0:T(8,128)S(1)} %copy-done), kind=kOutput, calls=%fused_computation.30 | convolution fusion | flops 402898944 | bytes 9502720 | tf_op jit(solution)/shard_map/bpc,bcd->bpd/dot_general | solution.py:50
  162.0 0.1 add_tanh_fusion
  162.1 0.0 collective-permute-done.4
  162.1 0.0 collective-permute-done.5
  162.1 3.7 %collective-permute-start.6 = (f32[34,1,128]{2,1,0:T(1,128)S(1)}, f32[34,1,128]{2,1,0:T(1,128)S(1)}, u32[]{:S(2)}, u32[]{:S(2)}) collective-permute-start(f32[34,1,128]{2,1,0:T(1,128)S(1)} %get-tuple-element.19), channel_id=1, source_target_pairs={{0,1},{1,2},{2,3},{3,4},{4,5},{5,6},{6,7},{8,9},{9,10},{10,11},{11... | collective-permute-start | bytes 52232 | tf_op jit(solution)/shard_map/ppermute | solution.py:19
  165.8 0.0 copy-start.3
  165.8 2.1 %collective-permute-start.7 = (f32[34,1,128]{2,1,0:T(1,128)S(1)}, f32[34,1,128]{2,1,0:T(1,128)S(1)}, u32[]{:S(2)}, u32[]{:S(2)}) collective-permute-start(f32[34,1,128]{2,1,0:T(1,128)S(1)} %get-tuple-element.20), channel_id=1, source_target_pairs={{1,0},{2,1},{3,2},{4,3},{5,4},{6,5},{7,6},{9,8},{10,9},{11,10},{12... | collective-permute-start | bytes 52232 | tf_op jit(solution)/shard_map/ppermute | solution.py:21
  167.9 0.2 pad_maximum_fusion.1
  168.1 1.0 fusion.26
  169.1 0.0 collective-permute-done.6
  169.1 2.1 %collective-permute-done.7 = f32[34,1,128]{2,1,0:T(1,128)S(1)} collective-permute-done((f32[34,1,128]{2,1,0:T(1,128)S(1)}, f32[34,1,128]{2,1,0:T(1,128)S(1)}, u32[]{:S(2)}, u32[]{:S(2)}) %collective-permute-start.7) | collective-permute-done | bytes 17440 | tf_op jit(solution)/shard_map/ppermute | solution.py:21
  171.2 0.2 maximum_maximum_fusion
  171.4 0.8 fusion.53
  172.2 1.0 fusion.9
  173.2 1.0 convolution_add_fusion.6
  174.2 1.0 convolution_add_fusion.5
  175.2 1.0 convolution_add_fusion.4
  176.2 1.0 convolution_add_fusion.3
  177.2 1.0 convolution_add_fusion.2
  178.2 1.0 convolution_add_fusion.1
  179.2 1.1 fusion
  180.3 0.2 broadcast_in_dim.76
  180.5 1.5 tanh_add_fusion
  (27 shorter events, 0.2 us)
Async XLA Ops:
  5.1 11.0 %copy-start.1 = (f32[32,64,128]{2,1,0:T(8,128)S(1)}, f32[32,64,128]{2,1,0:T(8,128)}, u32[]{:S(2)}) copy-start(f32[32,64,128]{2,1,0:T(8,128)} %param.9) | copy-start | bytes 3145732
  5.1 17.2 %copy-start.9 = (s32[128,1]{0,1:T(1,128)S(1)}, s32[128,1]{0,1:T(1,128)}, u32[]{:S(2)}) copy-start(s32[128,1]{0,1:T(1,128)} %param.12) | copy-start | bytes 1540
  5.1 17.2 %copy-start.8 = (f32[2,128]{1,0:T(2,128)S(1)}, f32[2,128]{1,0:T(2,128)}, u32[]{:S(2)}) copy-start(f32[2,128]{1,0:T(2,128)} %param.14) | copy-start | bytes 3076
  5.1 17.2 %copy-start.5 = (s32[2,8,16]{2,1,0:T(8,128)S(1)}, s32[2,8,16]{2,1,0:T(8,128)}, u32[]{:S(2)}) copy-start(s32[2,8,16]{2,1,0:T(8,128)} %param.11) | copy-start | bytes 3076
  5.1 17.3 %copy-start.4 = (s32[2,32,64]{2,1,0:T(8,128)S(1)}, s32[2,32,64]{2,1,0:T(8,128)}, u32[]{:S(2)}) copy-start(s32[2,32,64]{2,1,0:T(8,128)} %param.10) | copy-start | bytes 49156
  5.1 122.2 %all-to-all-start = ((f32[128,128,128]{2,1,0:T(8,128)}), f32[128,128,128]{2,1,0:T(8,128)}, u32[]{:S(2)}, u32[]{:S(2)}) async-start(f32[128,128,128]{2,1,0:T(8,128)} %stack.2), calls=%async_computation | async-start | bytes 16777216 | tf_op jit(solution)/shard_map/all_to_all | solution.py:76
  16.1 88.0 %collective-permute-start.1 = (f32[1,64,128]{2,1,0:T(8,128)S(1)}, f32[1,64,128]{2,1,0:T(8,128)S(1)}, u32[]{:S(2)}, u32[]{:S(2)}) collective-permute-start(f32[1,64,128]{2,1,0:T(8,128)S(1)} %get-tuple-element.33), channel_id=1, source_target_pairs={{8,0},{16,8},{24,16},{32,24},{40,32},{48,40},{56,48},{64,56},{72,6... | collective-permute-start | bytes 98312 | tf_op jit(solution)/shard_map/ppermute | solution.py:21
  20.4 82.5 %collective-permute-start = (f32[1,64,128]{2,1,0:T(8,128)S(1)}, f32[1,64,128]{2,1,0:T(8,128)S(1)}, u32[]{:S(2)}, u32[]{:S(2)}) collective-permute-start(f32[1,64,128]{2,1,0:T(8,128)S(1)} %get-tuple-element.34), channel_id=1, source_target_pairs={{0,8},{8,16},{16,24},{24,32},{32,40},{40,48},{48,56},{56,64},{64,7... | collective-permute-start | bytes 98312 | tf_op jit(solution)/shard_map/ppermute | solution.py:19
  102.9 13.6 %copy-start.2 = (f32[9,128,128]{2,1,0:T(8,128)S(1)}, f32[9,128,128]{2,1,0:T(8,128)}, u32[]{:S(2)}) copy-start(f32[9,128,128]{2,1,0:T(8,128)} %param.13) | copy-start | bytes 1769476
  104.5 13.9 %collective-permute-start.2 = (f32[34,1,128]{2,1,0:T(1,128)S(1)}, f32[34,1,128]{2,1,0:T(1,128)S(1)}, u32[]{:S(2)}, u32[]{:S(2)}) collective-permute-start(f32[34,1,128]{2,1,0:T(1,128)S(1)} %get-tuple-element.24), channel_id=1, source_target_pairs={{0,1},{1,2},{2,3},{3,4},{4,5},{5,6},{6,7},{8,9},{9,10},{10,11},{11... | collective-permute-start | bytes 52232 | tf_op jit(solution)/shard_map/ppermute | solution.py:19
  114.3 5.1 %collective-permute-start.3 = (f32[34,1,128]{2,1,0:T(1,128)S(1)}, f32[34,1,128]{2,1,0:T(1,128)S(1)}, u32[]{:S(2)}, u32[]{:S(2)}) collective-permute-start(f32[34,1,128]{2,1,0:T(1,128)S(1)} %get-tuple-element.25), channel_id=1, source_target_pairs={{1,0},{2,1},{3,2},{4,3},{5,4},{6,5},{7,6},{9,8},{10,9},{11,10},{12... | collective-permute-start | bytes 52232 | tf_op jit(solution)/shard_map/ppermute | solution.py:21
  135.0 10.6 %copy-start.6 = (f32[128]{0:T(128)S(1)}, f32[128]{0:T(128)}, u32[]{:S(2)}) copy-start(f32[128]{0:T(128)} %param.17) | copy-start | bytes 1540
  135.0 19.6 %copy-start = (f32[128,128,128]{2,1,0:T(8,128)S(1)}, f32[128,128,128]{2,1,0:T(8,128)}, u32[]{:S(2)}) copy-start(f32[128,128,128]{2,1,0:T(8,128)} %gather_fusion) | copy-start | bytes 25165828
  145.6 0.7 copy-start.7
  147.0 15.1 %collective-permute-start.4 = (f32[1,64,128]{2,1,0:T(8,128)S(1)}, f32[1,64,128]{2,1,0:T(8,128)S(1)}, u32[]{:S(2)}, u32[]{:S(2)}) collective-permute-start(f32[1,64,128]{2,1,0:T(8,128)S(1)} %get-tuple-element.28), channel_id=1, source_target_pairs={{0,8},{8,16},{16,24},{24,32},{32,40},{40,48},{48,56},{56,64},{64,7... | collective-permute-start | bytes 98312 | tf_op jit(solution)/shard_map/ppermute | solution.py:19
  149.1 13.0 %collective-permute-start.5 = (f32[1,64,128]{2,1,0:T(8,128)S(1)}, f32[1,64,128]{2,1,0:T(8,128)S(1)}, u32[]{:S(2)}, u32[]{:S(2)}) collective-permute-start(f32[1,64,128]{2,1,0:T(8,128)S(1)} %get-tuple-element.29), channel_id=1, source_target_pairs={{8,0},{16,8},{24,16},{32,24},{40,32},{48,40},{56,48},{64,56},{72,6... | collective-permute-start | bytes 98312 | tf_op jit(solution)/shard_map/ppermute | solution.py:21
  162.1 7.0 %collective-permute-start.6 = (f32[34,1,128]{2,1,0:T(1,128)S(1)}, f32[34,1,128]{2,1,0:T(1,128)S(1)}, u32[]{:S(2)}, u32[]{:S(2)}) collective-permute-start(f32[34,1,128]{2,1,0:T(1,128)S(1)} %get-tuple-element.19), channel_id=1, source_target_pairs={{0,1},{1,2},{2,3},{3,4},{4,5},{5,6},{6,7},{8,9},{9,10},{10,11},{11... | collective-permute-start | bytes 52232 | tf_op jit(solution)/shard_map/ppermute | solution.py:19
  165.8 2.3 %copy-start.3 = (f32[9,128,128]{2,1,0:T(8,128)S(1)}, f32[9,128,128]{2,1,0:T(8,128)}, u32[]{:S(2)}) copy-start(f32[9,128,128]{2,1,0:T(8,128)} %param.13) | copy-start | bytes 1769476
  165.8 5.4 %collective-permute-start.7 = (f32[34,1,128]{2,1,0:T(1,128)S(1)}, f32[34,1,128]{2,1,0:T(1,128)S(1)}, u32[]{:S(2)}, u32[]{:S(2)}) collective-permute-start(f32[34,1,128]{2,1,0:T(1,128)S(1)} %get-tuple-element.20), channel_id=1, source_target_pairs={{1,0},{2,1},{3,2},{4,3},{5,4},{6,5},{7,6},{9,8},{10,9},{11,10},{12... | collective-permute-start | bytes 52232 | tf_op jit(solution)/shard_map/ppermute | solution.py:21
